TPU v7x, 128 devices: a whole 4x4x4 slice. The times are simulated.
128 devices in a mesh: space: 64 (over x, y, z), sub: 2 (over core).
Axes of the slice: x: 4, y: 4, z: 4, core: 2. Of those that a mesh axis runs over, the one named last changes fastest.
Arguments:
- mode_rows: float32 [256, 1048576], P(None, ('space', 'sub')), as said below
- snapshots: float32 [3, 64, 1048576], P(None, None, ('space', 'sub')), as said below
- probe_fields: float32 [128, 1048576], P(None, ('space', 'sub')), as said below
- core_factor: float32 [256, 256], replicated, as said below
Outputs:
- new_modes: float32 [256, 1048576], P(None, ('space', 'sub'))
- new_core: float32 [256, 256], replicated
- captured: float32 [3, 256, 320], replicated
Inputs may be any that keep to these rules, and one draw needn't show every extreme that they name: `mode_rows`: rows of full rank, entries of order one. `snapshots`: fields of order one. `probe_fields`: fields of order one. `core_factor`: lower triangular with a positive diagonal.
All inputs are finite; a program needn't handle non-finite values.
Results may differ from a plain program's by a relative error of at most 0.0003.
Values sent between devices are 32-bit elements; how exact they have to be, the bound alone decides.
A program may use at most 128 MiB of HBM per device.

v0:
```python
import jax
import jax.numpy as jnp
from jax import lax
from jax.sharding import PartitionSpec as P

TURNS = 2
PRECISE = lax.Precision.HIGHEST


def row_inner(left, right):
    return lax.dot_general(left, right, (((1,), (1,)), ((), ())), precision=PRECISE)


def matmul_high(left, right):
    return jnp.dot(left, right, precision=PRECISE)


def block_cholesky(matrix):
    order = matrix.shape[0]
    width = 64
    lowered = jnp.zeros((order, order), jnp.float32)
    for start in range(0, order, width):
        finish = start + width
        done_rows = lowered[start:finish, :start]
        diag_block = matrix[start:finish, start:finish] - matmul_high(done_rows, done_rows.T)
        diag_factor = jnp.linalg.cholesky(diag_block)
        lowered = lowered.at[start:finish, start:finish].set(diag_factor)
        if finish < order:
            below = matrix[finish:, start:finish] - matmul_high(
                lowered[finish:, :start], done_rows.T
            )
            panel = jax.scipy.linalg.solve_triangular(diag_factor, below.T, lower=True).T
            lowered = lowered.at[finish:, start:finish].set(panel)
    return lowered


def update_core(core_now, projected, factor, turn_count):
    rank_count = core_now.shape[0]
    batch_count = factor.shape[0]
    upper = jnp.concatenate([core_now, projected], axis=1)
    bottom = jnp.concatenate([jnp.zeros((batch_count, rank_count), jnp.float32), factor.T], axis=1)
    stacked = jnp.concatenate([upper, bottom], axis=0)
    squared = matmul_high(stacked, stacked.T)
    rotation = jnp.eye(rank_count + batch_count, rank_count, dtype=jnp.float32)
    for sweep_index in range(turn_count):
        rotation = matmul_high(squared, rotation)
        lowered = block_cholesky(matmul_high(rotation.T, rotation))
        rotation = jax.scipy.linalg.solve_triangular(lowered, rotation.T, lower=True).T
    fresh_core = block_cholesky(matmul_high(rotation.T, matmul_high(squared, rotation)))
    return (rotation, fresh_core)


def orthonormalize(residual, volume):
    gram_local = row_inner(residual, residual)
    factor = block_cholesky(lax.psum(gram_local, ("space", "sub")) * volume)
    orthogonal = jax.scipy.linalg.solve_triangular(factor, residual, lower=True)
    return (factor, orthogonal)


def body(mode_rows, snapshots, probe_fields, core_factor):
    local_rows = mode_rows.shape[1]
    batch_count = snapshots.shape[0]
    batch_width = snapshots.shape[1]
    volume = 1.0 / (local_rows * lax.axis_size("space") * lax.axis_size("sub"))
    window = jnp.concatenate(
        [snapshots.reshape(batch_count * batch_width, local_rows), probe_fields], axis=0
    )
    basis_now = mode_rows
    core_now = core_factor
    captured = []
    for batch_index in range(batch_count):
        incoming = snapshots[batch_index]
        projected = lax.psum(row_inner(basis_now, incoming), ("space", "sub")) * volume
        residual = incoming - matmul_high(projected.T, basis_now)
        factor, orthogonal = orthonormalize(residual, volume)
        rotation, core_now = update_core(core_now, projected, factor, TURNS)
        basis_now = matmul_high(rotation.T, jnp.concatenate([basis_now, orthogonal], axis=0))
        captured.append(lax.psum(row_inner(basis_now, window), ("space", "sub")) * volume)
    return (basis_now, core_now, jnp.stack(captured))


def solution(mesh):
    return jax.shard_map(
        body,
        mesh=mesh,
        in_specs=(
            P(None, ("space", "sub")),
            P(None, None, ("space", "sub")),
            P(None, ("space", "sub")),
            P(),
        ),
        out_specs=(P(None, ("space", "sub")), P(), P()),
        check_vma=False,
    )
```

profile of v0, /device:TPU:1, one launch (start us, length us, event | category | flops | bytes accessed | tf_op | source)
XLA Modules:
  0.0 1623.2 jit_solution(15675498892306487198)
XLA Ops:
  7.2 10.0 fusion.19
  17.3 143.2 %all-reduce.18.cloned.1.call-done = f32[256,64]{1,0:T(8,128)} async-done(((f32[256,64]{1,0:T(8,128)}), f32[256,64]{1,0:T(8,128)}) %all-reduce.18.cloned.1.call-update) | async-done | bytes 65552 | tf_op jit(solution)/shard_map/psum | solution.py:73
  160.5 9.2 convolution_subtract_fusion.2
  171.5 63.6 %psum.64 = f32[64,64]{0,1:T(8,128)S(1)} all-reduce(f32[64,64]{0,1:T(8,128)S(1)} %fusion.442), channel_id=1, replica_groups=mesh['space'=64,'sub'=2] {'space','sub'}, use_global_device_ids=true, to_apply=%region_1.0 | all-reduce | flops 4096 | bytes 32768 | tf_op jit(solution)/shard_map/psum | solution.py:55
  235.2 5.8 cholesky.599
  245.5 5.8 cholesky.610
  258.9 5.8 cholesky.621
  308.2 20.1 %custom-call.51 = f32[2,128,128]{1,2,0:T(8,128)S(1)} custom-call(f32[2,128,128]{2,1,0:T(8,128)S(1)} %get-tuple-element.863), custom_call_target="InvertDiagBlocksLowerTriangular" | custom-call | tf_op jit(solution)/shard_map/jit(_solve_triangular)/triangular_solve | solution.py:48
  330.9 5.8 cholesky.654
  344.3 5.8 cholesky.665
  365.9 5.8 cholesky.676
  384.1 5.8 cholesky.687
  398.1 19.8 %custom-call.55 = f32[2,128,128]{1,2,0:T(8,128)S(1)} custom-call(f32[2,128,128]{2,1,0:T(8,128)S(1)} %get-tuple-element.864), custom_call_target="InvertDiagBlocksLowerTriangular" | custom-call | tf_op jit(solution)/shard_map/jit(_solve_triangular)/triangular_solve | solution.py:48
  420.5 5.8 cholesky.698
  433.3 5.8 cholesky.709
  459.8 5.8 cholesky.720
  480.7 16.3 %fusion = f32[256,8192]{1,0:T(8,128)S(1)} fusion(f32[64,8192]{1,0:T(8,128)} %fusion.189, f32[256,8192]{1,0:T(8,128)} %param.153, f32[128,320]{0,1:T(8,128)S(1)} %fusion.125, f32[128,320]{0,1:T(8,128)S(1)} %fusion.98), kind=kOutput, calls=%fused_computation.12 | convolution fusion | flops 8055767040 | bytes 19202048 | tf_op jit(solution)/shard_map/dot_general | solution.py:15
  500.4 8.9 fusion.17
  509.3 13.3 fusion.14
  524.3 122.0 %all-reduce.20.cloned.1.call-done = f32[256,64]{1,0:T(8,128)} async-done(((f32[256,64]{1,0:T(8,128)}), f32[256,64]{1,0:T(8,128)}) %all-reduce.20.cloned.1.call-update) | async-done | bytes 65552 | tf_op jit(solution)/shard_map/psum | solution.py:73
  646.3 9.2 convolution_subtract_fusion.1
  657.2 63.7 %psum.66 = f32[64,64]{0,1:T(8,128)S(1)} all-reduce(f32[64,64]{0,1:T(8,128)S(1)} %fusion.445), channel_id=1, replica_groups=mesh['space'=64,'sub'=2] {'space','sub'}, use_global_device_ids=true, to_apply=%region_5.12 | all-reduce | flops 4096 | bytes 32768 | tf_op jit(solution)/shard_map/psum | solution.py:55
  721.0 5.8 cholesky.742
  731.3 5.8 cholesky.753
  744.8 5.8 cholesky.764
  766.3 5.8 cholesky.775
  782.2 5.8 cholesky.786
  794.5 19.8 %custom-call.63 = f32[2,128,128]{1,2,0:T(8,128)S(1)} custom-call(f32[2,128,128]{2,1,0:T(8,128)S(1)} %get-tuple-element.865), custom_call_target="InvertDiagBlocksLowerTriangular" | custom-call | tf_op jit(solution)/shard_map/jit(_solve_triangular)/triangular_solve | solution.py:48
  816.9 5.8 cholesky.797
  830.4 5.8 cholesky.808
  852.1 5.8 cholesky.819
  870.4 5.8 cholesky.830
  884.3 19.9 %custom-call.67 = f32[2,128,128]{1,2,0:T(8,128)S(1)} custom-call(f32[2,128,128]{2,1,0:T(8,128)S(1)} %get-tuple-element.866), custom_call_target="InvertDiagBlocksLowerTriangular" | custom-call | tf_op jit(solution)/shard_map/jit(_solve_triangular)/triangular_solve | solution.py:48
  906.7 5.8 cholesky.841
  944.9 17.2 %fusion.4 = f32[256,8192]{1,0:T(8,128)S(1)} fusion(f32[64,8192]{1,0:T(8,128)S(1)} %fusion.165, f32[256,8192]{1,0:T(8,128)} %copy-done.1, f32[128,320]{0,1:T(8,128)S(1)} %fusion.115, f32[128,320]{0,1:T(8,128)S(1)} %fusion.94), kind=kOutput, calls=%fused_computation.16 | convolution fusion | flops 8055767040 | bytes 19202048 | tf_op jit(solution)/shard_map/dot_general | solution.py:15
  965.3 8.9 fusion.15
  974.2 13.1 fusion.13
  1010.1 114.5 %all-reduce.22.cloned.1.call-done = f32[256,64]{1,0:T(8,128)} async-done(((f32[256,64]{1,0:T(8,128)}), f32[256,64]{1,0:T(8,128)}) %all-reduce.22.cloned.1.call-update) | async-done | bytes 65552 | tf_op jit(solution)/shard_map/psum | solution.py:73
  1124.6 9.2 convolution_subtract_fusion
  1135.6 63.8 %psum.68 = f32[64,64]{0,1:T(8,128)S(1)} all-reduce(f32[64,64]{0,1:T(8,128)S(1)} %fusion.448), channel_id=1, replica_groups=mesh['space'=64,'sub'=2] {'space','sub'}, use_global_device_ids=true, to_apply=%region_7.14 | all-reduce | flops 4096 | bytes 32768 | tf_op jit(solution)/shard_map/psum | solution.py:55
  1209.8 5.8 cholesky.896
  1272.4 19.9 %custom-call.75 = f32[2,128,128]{1,2,0:T(8,128)S(1)} custom-call(f32[2,128,128]{2,1,0:T(8,128)S(1)} %get-tuple-element.867), custom_call_target="InvertDiagBlocksLowerTriangular" | custom-call | tf_op jit(solution)/shard_map/jit(_solve_triangular)/triangular_solve | solution.py:48
  1294.9 5.8 cholesky.940
  1362.3 20.1 %custom-call.79 = f32[2,128,128]{1,2,0:T(8,128)S(1)} custom-call(f32[2,128,128]{2,1,0:T(8,128)S(1)} %get-tuple-element.868), custom_call_target="InvertDiagBlocksLowerTriangular" | custom-call | tf_op jit(solution)/shard_map/jit(_solve_triangular)/triangular_solve | solution.py:48
  1384.9 5.8 cholesky.984
  1422.8 18.3 %fusion.8 = f32[256,8192]{1,0:T(8,128)} fusion(f32[64,8192]{1,0:T(8,128)S(1)} %fusion.148, f32[256,8192]{1,0:T(8,128)} %copy-done, f32[128,320]{0,1:T(8,128)S(1)} %fusion.105, f32[128,320]{0,1:T(8,128)S(1)} %fusion.90), kind=kOutput, calls=%fused_computation.20 | convolution fusion | flops 8055767040 | bytes 19202048 | tf_op jit(solution)/shard_map/dot_general | solution.py:15
  1455.7 13.1 fusion.12
  1477.1 136.2 %all-reduce.24.cloned.1.call-done = (f32[256,320]{0,1:T(8,128)}, f32[256,320]{0,1:T(8,128)}, f32[256,320]{0,1:T(8,128)}) async-done(((f32[256,320]{0,1:T(8,128)}, f32[256,320]{0,1:T(8,128)}, f32[256,320]{0,1:T(8,128)}), (f32[256,320]{0,1:T(8,128)}, f32[256,320]{0,1:T(8,128)}, f32[256,320]{0,1:T(8,128)})) %all-reduce.24.cloned.1.call-update) | async-done | bytes 983056 | tf_op jit(solution)/shard_map/psum | solution.py:78
  (535 shorter events, 522.5 us)
Async XLA Ops:
  7.2 153.3 %all-reduce.18.cloned.1.call-start = ((), (), s32[]{:S(2)}) async-start(), calls=%async_computation | async-start | bytes 262144 | tf_op jit(solution)/shard_map/psum | solution.py:73
  17.2 629.1 %all-reduce.20.cloned.1.call-start = ((), (), s32[]{:S(2)}) async-start(), calls=%async_computation.1 | async-start | bytes 262144 | tf_op jit(solution)/shard_map/psum | solution.py:73
  17.3 225.8 %copy-start.9 = (f32[256,256]{1,0:T(8,128)S(1)}, f32[256,256]{1,0:T(8,128)}, u32[]{:S(2)}) copy-start(f32[256,256]{1,0:T(8,128)} %param.156) | copy-start | bytes 786436
  160.5 82.5 %copy-start.6 = (f32[256,64]{1,0:T(8,128)S(1)}, f32[256,64]{1,0:T(8,128)}, u32[]{:S(2)}) copy-start(f32[256,64]{1,0:T(8,128)} %all-reduce.18.cloned.1.call-done) | copy-start | bytes 196612
  245.4 34.5 %copy-start.2 = (f32[256,256]{0,1:T(8,128)}, f32[256,256]{0,1:T(8,128)S(1)}, u32[]{:S(2)}) copy-start(f32[256,256]{0,1:T(8,128)S(1)} %fusion.443) | copy-start | bytes 786436
  497.0 3.4 copy-start.1
  509.3 615.3 %all-reduce.22.cloned.1.call-start = ((), (), s32[]{:S(2)}) async-start(), calls=%async_computation.2 | async-start | bytes 262144 | tf_op jit(solution)/shard_map/psum | solution.py:73
  646.3 82.6 %copy-start.7 = (f32[256,64]{1,0:T(8,128)S(1)}, f32[256,64]{1,0:T(8,128)}, u32[]{:S(2)}) copy-start(f32[256,64]{1,0:T(8,128)} %all-reduce.20.cloned.1.call-done) | copy-start | bytes 196612
  731.2 34.8 %copy-start.3 = (f32[256,256]{0,1:T(8,128)}, f32[256,256]{0,1:T(8,128)S(1)}, u32[]{:S(2)}) copy-start(f32[256,256]{0,1:T(8,128)S(1)} %fusion.446) | copy-start | bytes 786436
  962.1 3.2 copy-start
  987.3 626.0 %all-reduce.24.cloned.1.call-start = ((), (), s32[]{:S(2)}) async-start(), calls=%async_computation.3 | async-start | bytes 1966080 | tf_op jit(solution)/shard_map/psum | solution.py:78
  1124.6 82.8 %copy-start.5 = (f32[256,64]{1,0:T(8,128)S(1)}, f32[256,64]{1,0:T(8,128)}, u32[]{:S(2)}) copy-start(f32[256,64]{1,0:T(8,128)} %all-reduce.22.cloned.1.call-done) | copy-start | bytes 196612
  1209.7 34.4 %copy-start.4 = (f32[256,256]{0,1:T(8,128)}, f32[256,256]{0,1:T(8,128)S(1)}, u32[]{:S(2)}) copy-start(f32[256,256]{0,1:T(8,128)S(1)} %fusion.449) | copy-start | bytes 786436
  1477.0 139.4 %copy-start.8 = (f32[256,256]{1,0:T(8,128)}, f32[256,256]{1,0:T(8,128)S(1)}, u32[]{:S(2)}) copy-start(f32[256,256]{1,0:T(8,128)S(1)} %scatter.314) | copy-start | bytes 786436
Sparse Core Ops, SparseCore 0:
  17.3 143.1 all-reduce.17
  509.4 136.8 all-reduce.19
  987.5 137.0 all-reduce.21
  1469.0 144.2 all-reduce.23
where the time goes:
time: 1630 us; the launch traced here: 1620 us
  other arithmetic  568 us (35%)
  waiting for transfers between devices  516 us (32%)
  matrix products  212 us (13%)
  blocking collectives  191 us (12%)
  local copies, waits for them, and re-layouts  118 us (7%)
  between operations  16.6 us (1%)
    psum x3, waiting for transfers between devices, body(): lax.psum(row_inner(basis_now, incoming), ('space', 'sub')) * volume  380 us
    another operation x117, other arithmetic, block_cholesky(): diag_factor = jnp.linalg.cholesky(diag_block)  255 us
    psum x3, blocking collectives, orthonormalize(): factor = block_cholesky(lax.psum(gram_local, ('space', 'sub')) * volume)  191 us
    another operation x54, other arithmetic, block_cholesky(): jax.scipy.linalg.solve_triangular(diag_factor, below.T, lower=True)  161 us
    psum x1, waiting for transfers between devices, body(): lax.psum(row_inner(basis_now, window), ('space', 'sub')) * volume  136 us
    another operation x13, other arithmetic, update_core(): jax.scipy.linalg.solve_triangular(lowered, rotation.T, lower=True)  123 us
    dot_general x72, matrix products, matmul_high(): return jnp.dot(left, right, precision=PRECISE)  114 us
    dot_general x9, matrix products, row_inner(): lax.dot_general(left, right, (((1,), (1,)), ((), ())), precision=PRECISE)  72.7 us
  transfers between devices with their start and end apart: 4, of which 4 were waited for; matrix products, arithmetic and copies ran while one was open for 3% of the time, Pallas kernels for 0%

commit v1 on v0

--- a/solution.py
+++ b/solution.py
@@ -2,6 +2,7 @@
 import jax.numpy as jnp
 from jax import lax
 from jax.sharding import PartitionSpec as P
+from jax.lax import all_gather
 
 TURNS = 2
 PRECISE = lax.Precision.HIGHEST
@@ -70,7 +71,9 @@
     captured = []
     for batch_index in range(batch_count):
         incoming = snapshots[batch_index]
-        projected = lax.psum(row_inner(basis_now, incoming), ("space", "sub")) * volume
+        projected = (
+            all_gather(row_inner(basis_now, incoming), ("space", "sub")).sum(axis=0) * volume
+        )
         residual = incoming - matmul_high(projected.T, basis_now)
         factor, orthogonal = orthonormalize(residual, volume)
         rotation, core_now = update_core(core_now, projected, factor, TURNS)

time: 1630 us -> 1370 us (0.84)
  waiting for transfers between devices: 516 us -> 232 us
    psum x3 -> x0, waiting for transfers between devices: 380 us -> none  [body(): lax.psum(row_inner(basis_now, incoming), ('space', 'sub')) * volume]
    all_gather x0 -> x3, waiting for transfers between devices: none -> 96 us  [body(): all_gather(row_inner(basis_now, incoming), ('space', 'sub')).sum(axis=0)]
  transfers between devices with their start and end apart: 4 -> 4, of which waited for: 4 -> 3; matrix products, arithmetic and copies ran while one was open for 3% -> 11% of each run, Pallas kernels for 0% -> 0%
where the time goes in v1:
time: 1370 us; the launch traced here: 1360 us
  other arithmetic  571 us (42%)
  waiting for transfers between devices  232 us (17%)
  matrix products  216 us (16%)
  blocking collectives  194 us (14%)
  local copies, waits for them, and re-layouts  129 us (9%)
  between operations  16.7 us (1%)
    another operation x117, other arithmetic, block_cholesky(): diag_factor = jnp.linalg.cholesky(diag_block)  255 us
    psum x3, blocking collectives, orthonormalize(): factor = block_cholesky(lax.psum(gram_local, ('space', 'sub')) * volume)  194 us
    another operation x54, other arithmetic, block_cholesky(): jax.scipy.linalg.solve_triangular(diag_factor, below.T, lower=True)  161 us
    psum x1, waiting for transfers between devices, body(): lax.psum(row_inner(basis_now, window), ('space', 'sub')) * volume  136 us
    another operation x13, other arithmetic, update_core(): jax.scipy.linalg.solve_triangular(lowered, rotation.T, lower=True)  121 us
    dot_general x72, matrix products, matmul_high(): return jnp.dot(left, right, precision=PRECISE)  112 us
    all_gather x3, waiting for transfers between devices, body(): all_gather(row_inner(basis_now, incoming), ('space', 'sub')).sum(axis=0)  96 us
    dot_general x9, matrix products, row_inner(): lax.dot_general(left, right, (((1,), (1,)), ((), ())), precision=PRECISE)  77.5 us
  transfers between devices with their start and end apart: 4, of which 3 were waited for; matrix products, arithmetic and copies ran while one was open for 11% of the time, Pallas kernels for 0%

profile of v1, /device:TPU:1, one launch (start us, length us, event | category | flops | bytes accessed | tf_op | source)
XLA Modules:
  0.0 1359.5 jit_solution(2844324064561321461)
XLA Ops:
  7.2 12.3 fusion.19
  19.8 77.9 %all-gather.7.cloned.1.call-done = f32[32768,64]{0,1:T(8,128)} async-done(((f32[256,64]{0,1:T(8,128)}), f32[32768,64]{0,1:T(8,128)}) %all-gather.7.cloned.1.call-update) | async-done | bytes 8388624 | tf_op jit(solution)/shard_map/all_gather | solution.py:75
  97.7 5.9 copy.247
  105.2 9.1 convolution_subtract_fusion.2
  116.1 64.6 %psum.42 = f32[64,64]{0,1:T(8,128)S(1)} all-reduce(f32[64,64]{0,1:T(8,128)S(1)} %fusion.442), channel_id=1, replica_groups=mesh['space'=64,'sub'=2] {'space','sub'}, use_global_device_ids=true, to_apply=%region_1.0 | all-reduce | flops 4096 | bytes 32768 | tf_op jit(solution)/shard_map/psum | solution.py:56
  180.8 5.8 cholesky.599
  191.1 5.8 cholesky.610
  204.6 5.8 cholesky.621
  225.9 5.8 cholesky.632
  241.8 5.8 cholesky.643
  254.0 20.1 %custom-call.51 = f32[2,128,128]{1,2,0:T(8,128)S(1)} custom-call(f32[2,128,128]{2,1,0:T(8,128)S(1)} %get-tuple-element.863), custom_call_target="InvertDiagBlocksLowerTriangular" | custom-call | tf_op jit(solution)/shard_map/jit(_solve_triangular)/triangular_solve | solution.py:49
  276.7 5.8 cholesky.654
  290.3 5.8 cholesky.665
  320.4 5.8 cholesky.676
  336.2 5.8 cholesky.687
  348.4 19.7 %custom-call.55 = f32[2,128,128]{1,2,0:T(8,128)S(1)} custom-call(f32[2,128,128]{2,1,0:T(8,128)S(1)} %get-tuple-element.864), custom_call_target="InvertDiagBlocksLowerTriangular" | custom-call | tf_op jit(solution)/shard_map/jit(_solve_triangular)/triangular_solve | solution.py:49
  369.0 16.1 %fusion = f32[256,8192]{1,0:T(8,128)S(1)} fusion(f32[64,8192]{1,0:T(8,128)} %fusion.189, f32[256,8192]{1,0:T(8,128)} %param.153, f32[128,320]{0,1:T(8,128)S(1)} %fusion.125, f32[128,320]{0,1:T(8,128)S(1)} %fusion.98), kind=kOutput, calls=%fused_computation.12 | convolution fusion | flops 8055767040 | bytes 19202048 | tf_op jit(solution)/shard_map/dot_general | solution.py:16
  388.5 10.0 fusion.17
  400.2 5.8 cholesky.698
  413.0 5.9 cholesky.709
  430.8 5.8 cholesky.720
  445.1 5.8 cholesky.731
  453.3 18.1 %all-gather.9.cloned.1.call-done = f32[32768,64]{0,1:T(8,128)} async-done(((f32[256,64]{0,1:T(8,128)}), f32[32768,64]{0,1:T(8,128)}) %all-gather.9.cloned.1.call-update) | async-done | bytes 8388624 | tf_op jit(solution)/shard_map/all_gather | solution.py:75
  471.4 5.9 copy.248
  479.1 9.1 convolution_subtract_fusion.1
  490.0 64.5 %psum.43 = f32[64,64]{0,1:T(8,128)S(1)} all-reduce(f32[64,64]{0,1:T(8,128)S(1)} %fusion.445), channel_id=1, replica_groups=mesh['space'=64,'sub'=2] {'space','sub'}, use_global_device_ids=true, to_apply=%region_5.12 | all-reduce | flops 4096 | bytes 32768 | tf_op jit(solution)/shard_map/psum | solution.py:56
  554.5 5.8 cholesky.742
  564.8 5.8 cholesky.753
  578.2 5.8 cholesky.764
  627.8 20.1 %custom-call.63 = f32[2,128,128]{1,2,0:T(8,128)S(1)} custom-call(f32[2,128,128]{2,1,0:T(8,128)S(1)} %get-tuple-element.865), custom_call_target="InvertDiagBlocksLowerTriangular" | custom-call | tf_op jit(solution)/shard_map/jit(_solve_triangular)/triangular_solve | solution.py:49
  650.5 5.8 cholesky.797
  722.0 19.7 %custom-call.67 = f32[2,128,128]{1,2,0:T(8,128)S(1)} custom-call(f32[2,128,128]{2,1,0:T(8,128)S(1)} %get-tuple-element.866), custom_call_target="InvertDiagBlocksLowerTriangular" | custom-call | tf_op jit(solution)/shard_map/jit(_solve_triangular)/triangular_solve | solution.py:49
  742.6 16.1 %fusion.4 = f32[256,8192]{1,0:T(8,128)S(1)} fusion(f32[64,8192]{1,0:T(8,128)} %fusion.165, f32[256,8192]{1,0:T(8,128)} %copy-done.1, f32[128,320]{0,1:T(8,128)S(1)} %fusion.115, f32[128,320]{0,1:T(8,128)S(1)} %fusion.94), kind=kOutput, calls=%fused_computation.16 | convolution fusion | flops 8055767040 | bytes 19202048 | tf_op jit(solution)/shard_map/dot_general | solution.py:16
  762.0 10.0 fusion.15
  772.0 13.5 fusion.14
  787.2 5.8 cholesky.841
  840.0 13.3 fusion.13
  853.3 5.9 copy.249
  861.0 9.1 convolution_subtract_fusion
  871.9 64.5 %psum.44 = f32[64,64]{0,1:T(8,128)S(1)} all-reduce(f32[64,64]{0,1:T(8,128)S(1)} %fusion.448), channel_id=1, replica_groups=mesh['space'=64,'sub'=2] {'space','sub'}, use_global_device_ids=true, to_apply=%region_7.14 | all-reduce | flops 4096 | bytes 32768 | tf_op jit(solution)/shard_map/psum | solution.py:56
  946.9 5.8 cholesky.896
  1009.4 19.9 %custom-call.75 = f32[2,128,128]{1,2,0:T(8,128)S(1)} custom-call(f32[2,128,128]{2,1,0:T(8,128)S(1)} %get-tuple-element.867), custom_call_target="InvertDiagBlocksLowerTriangular" | custom-call | tf_op jit(solution)/shard_map/jit(_solve_triangular)/triangular_solve | solution.py:49
  1031.8 5.8 cholesky.940
  1099.0 20.1 %custom-call.79 = f32[2,128,128]{1,2,0:T(8,128)S(1)} custom-call(f32[2,128,128]{2,1,0:T(8,128)S(1)} %get-tuple-element.868), custom_call_target="InvertDiagBlocksLowerTriangular" | custom-call | tf_op jit(solution)/shard_map/jit(_solve_triangular)/triangular_solve | solution.py:49
  1121.6 5.8 cholesky.984
  1159.5 18.3 %fusion.8 = f32[256,8192]{1,0:T(8,128)} fusion(f32[64,8192]{1,0:T(8,128)S(1)} %fusion.148, f32[256,8192]{1,0:T(8,128)} %copy-done, f32[128,320]{0,1:T(8,128)S(1)} %fusion.105, f32[128,320]{0,1:T(8,128)S(1)} %fusion.90), kind=kOutput, calls=%fused_computation.20 | convolution fusion | flops 8055767040 | bytes 19202048 | tf_op jit(solution)/shard_map/dot_general | solution.py:16
  1192.4 13.1 fusion.12
  1213.8 135.9 %all-reduce.15.cloned.1.call-done = (f32[256,320]{0,1:T(8,128)}, f32[256,320]{0,1:T(8,128)}, f32[256,320]{0,1:T(8,128)}) async-done(((f32[256,320]{0,1:T(8,128)}, f32[256,320]{0,1:T(8,128)}, f32[256,320]{0,1:T(8,128)}), (f32[256,320]{0,1:T(8,128)}, f32[256,320]{0,1:T(8,128)}, f32[256,320]{0,1:T(8,128)})) %all-reduce.15.cloned.1.call-update) | async-done | bytes 983056 | tf_op jit(solution)/shard_map/psum | solution.py:81
  (542 shorter events, 531.0 us)
Async XLA Ops:
  7.2 90.5 %all-gather.7.cloned.1.call-start = ((), (), s32[]{:S(2)}) async-start(), calls=%async_computation | async-start | bytes 8454144 | tf_op jit(solution)/shard_map/all_gather | solution.py:75
  19.6 451.8 %all-gather.9.cloned.1.call-start = ((), (), s32[]{:S(2)}) async-start(), calls=%async_computation.1 | async-start | bytes 8454144 | tf_op jit(solution)/shard_map/all_gather | solution.py:75
  105.2 83.5 %copy-start.8 = (f32[256,256]{1,0:T(8,128)S(1)}, f32[256,256]{1,0:T(8,128)}, u32[]{:S(2)}) copy-start(f32[256,256]{1,0:T(8,128)} %param.156) | copy-start | bytes 786436
  191.0 34.6 %copy-start.4 = (f32[256,256]{0,1:T(8,128)}, f32[256,256]{0,1:T(8,128)S(1)}, u32[]{:S(2)}) copy-start(f32[256,256]{0,1:T(8,128)S(1)} %fusion.443) | copy-start | bytes 786436
  276.6 34.6 %copy-start.2 = (f32[256,256]{0,1:T(8,128)}, f32[256,256]{0,1:T(8,128)S(1)}, u32[]{:S(2)}) copy-start(f32[256,256]{0,1:T(8,128)S(1)} %fusion.444) | copy-start | bytes 786436
  385.1 3.4 copy-start.1
  398.5 454.8 %all-gather.11.cloned.1.call-start = ((), (), s32[]{:S(2)}) async-start(), calls=%async_computation.2 | async-start | bytes 8454144 | tf_op jit(solution)/shard_map/all_gather | solution.py:75
  564.7 34.5 %copy-start.5 = (f32[256,256]{0,1:T(8,128)}, f32[256,256]{0,1:T(8,128)S(1)}, u32[]{:S(2)}) copy-start(f32[256,256]{0,1:T(8,128)S(1)} %fusion.446) | copy-start | bytes 786436
  650.4 34.4 %copy-start.3 = (f32[256,256]{0,1:T(8,128)}, f32[256,256]{0,1:T(8,128)S(1)}, u32[]{:S(2)}) copy-start(f32[256,256]{0,1:T(8,128)S(1)} %fusion.447) | copy-start | bytes 786436
  758.7 3.2 copy-start
  771.9 577.7 %all-reduce.15.cloned.1.call-start = ((), (), s32[]{:S(2)}) async-start(), calls=%async_computation.3 | async-start | bytes 1966080 | tf_op jit(solution)/shard_map/psum | solution.py:81
  946.7 34.3 %copy-start.6 = (f32[256,256]{0,1:T(8,128)}, f32[256,256]{0,1:T(8,128)S(1)}, u32[]{:S(2)}) copy-start(f32[256,256]{0,1:T(8,128)S(1)} %fusion.449) | copy-start | bytes 786436
  1213.7 139.0 %copy-start.7 = (f32[256,256]{1,0:T(8,128)}, f32[256,256]{1,0:T(8,128)S(1)}, u32[]{:S(2)}) copy-start(f32[256,256]{1,0:T(8,128)S(1)} %scatter.314) | copy-start | bytes 786436
Sparse Core Ops, SparseCore 0:
  19.7 77.9 all-gather.6
  398.6 72.7 all-gather.8
  772.1 72.4 all-gather.10
  1205.7 143.8 all-reduce.14
